TPU v7x, 32 devices: a whole 2x2x4 slice. The times are simulated.
32 devices in a mesh: dp: 8 (over z, x), shard: 4 (over y, core).
Axes of the slice: x: 2, y: 2, z: 4, core: 2. Of those that a mesh axis runs over, the one named last changes fastest.
Arguments:
- grads: bfloat16 [8, 384, 8192], P('dp', 'shard'), may hold values from -6 to 6
- momentum: float32 [8, 384, 8192], P('dp', 'shard'), may hold values from -6 to 6
- param: float32 [384, 8192], P('shard'), may hold values from -6 to 6
- thresholds: float32 [384], P('shard'), may hold values from 0.1 to 1
- sel_blocks: int32 [8, 4, 768], P(None, 'shard'), may hold values from 0 to 6143, as said below
- counts: int32 [8, 4], P(None, 'shard'), may hold values from 192 to 768, as said below
Outputs:
- new_momentum: float32 [8, 384, 8192], P('dp', 'shard')
- new_param: float32 [384, 8192], P('shard')
- compute_copy: bfloat16 [384, 8192], replicated
Inputs may be any that keep to these rules, and one draw needn't show every extreme that they name: `sel_blocks`: within one replica and shard the 768 entries are distinct block numbers of that shard. `counts`: some replica has 768 live slots in every shard.
All inputs are finite; a program needn't handle non-finite values.
Results may differ from a plain program's by a relative error of at most 0.0019.
Values may be sent and summed in bfloat16 or wider, within the bound.
A program may use at most 128 MiB of HBM per device.

v0:
```python
import functools

import jax
import jax.numpy as jnp
import numpy as np
from jax import lax
from jax.experimental import pallas as pl
from jax.experimental.pallas import tpu as pltpu
from jax.sharding import PartitionSpec as P

BLK = 128
HALF = 64
beta_decay = 0.999
step_size = 0.1
UNROLL = 16


def tables():
    pos = np.arange(BLK)
    sample, freq = (pos % HALF)[:, None], (pos % HALF)[None, :]
    same = pos[:, None] // HALF == pos[None, :] // HALF
    weights = np.where(freq == 0, np.sqrt(1.0 / HALF), np.sqrt(2.0 / HALF))
    table = np.where(same, weights * np.cos((2 * sample + 1) * freq * (np.pi / BLK)), 0.0).astype(np.float32)

    def wide(t):
        hi = t.astype(jnp.bfloat16)
        lo = (t - hi.astype(np.float32)).astype(jnp.bfloat16)
        half = np.concatenate([hi, lo], axis=1)
        return np.concatenate([half, half], axis=0)

    return wide(table), wide(table.T)


def split(x):
    hi = x.astype(jnp.bfloat16)
    lo = (x - hi.astype(jnp.float32)).astype(jnp.bfloat16)
    return jnp.concatenate([hi, lo], axis=1)


def both(x, w):
    y = jnp.dot(x, w, preferred_element_type=jnp.float32)
    return y[:, :BLK] + y[:, BLK:]


def tiles(x):
    return jnp.concatenate([x[:, c * BLK : (c + 1) * BLK] for c in range(x.shape[1] // BLK)], axis=0)


def encode_kernel(per_row, mom, grad, thr, sel, place, counts, fwd, inv, newmom, sent, rowhot, dense, picked, level):
    step = pl.program_id(0)
    replica = lax.axis_index("dp")
    rows, width = mom.shape
    slots = sel.shape[2]
    cols = width // BLK
    ids = sel[replica]

    @pl.when(step == 0)
    def _():
        live = lax.broadcasted_iota(jnp.int32, (1, slots), 1) < counts[replica]
        row_of = jnp.where(live, ids // per_row, -1)
        hot = row_of == lax.broadcasted_iota(jnp.int32, (rows, slots), 0)
        rowhot[...] = jnp.where(hot, 1.0, 0.0).astype(jnp.bfloat16)
        eye = lax.broadcasted_iota(jnp.int32, (rows, rows), 0) == lax.broadcasted_iota(jnp.int32, (rows, rows), 1)
        column = jnp.sum(jnp.where(eye, thr[...], 0.0), axis=1, keepdims=True)
        level[...] = jnp.broadcast_to(column, level.shape)

    colhot = ids % per_row == step * cols + lax.broadcasted_iota(jnp.int32, (max(cols, 8), slots), 0)
    mask = lax.dot_general(
        rowhot[...],
        jnp.where(colhot, 1.0, 0.0).astype(jnp.bfloat16),
        (((1,), (1,)), ((), ())),
        preferred_element_type=jnp.float32,
    )
    blended = tiles(beta_decay * mom[...] + grad[...].astype(jnp.float32))
    coef = both(split(blended), fwd[...])
    t = jnp.concatenate([level[...]] * cols, axis=0)
    shrunk = coef - jnp.clip(coef, -t, t)
    keep = jnp.concatenate([jnp.broadcast_to(mask[:, c : c + 1], (rows, BLK)) for c in range(cols)], axis=0)
    kept = jnp.where(keep > 0.5, shrunk, 0.0)
    for c in range(cols):
        dense[pl.ds(step * cols + c, rows, stride=per_row), :] = kept[c * rows : (c + 1) * rows]
    out = blended - both(kept.astype(jnp.bfloat16), inv[:BLK, :])
    for c in range(cols):
        newmom[:, c * BLK : (c + 1) * BLK] = out[c * rows : (c + 1) * rows]

    @pl.when(step == pl.num_programs(0) - 1)
    def _():
        def pick(i, carry):
            base = i * UNROLL
            got = [dense[pl.ds(place[replica, 0, base + u], 1), :] for u in range(UNROLL)]
            for u in range(UNROLL):
                picked[pl.ds(base + u, 1), :] = got[u]
            return carry

        lax.fori_loop(0, slots // UNROLL, pick, 0)
        sent[...] = picked[...].astype(jnp.bfloat16)


def encode(mom, grad, thr, sel, counts, fwd, inv, width):
    rows, D = mom.shape
    slots = sel.shape[2]
    col = pl.BlockSpec((rows, width), lambda i: (0, i))
    whole = lambda a: pl.BlockSpec(a.shape, lambda i: (0,) * a.ndim)
    smem = pl.BlockSpec(memory_space=pltpu.SMEM)
    return pl.pallas_call(
        functools.partial(encode_kernel, D // BLK),
        grid=(D // width,),
        in_specs=[col, col, whole(thr), whole(sel), smem, smem, whole(fwd), whole(inv)],
        out_specs=[col, pl.BlockSpec((slots, BLK), lambda i: (0, 0))],
        out_shape=[
            jax.ShapeDtypeStruct(mom.shape, jnp.float32),
            jax.ShapeDtypeStruct((slots, BLK), jnp.bfloat16),
        ],
        scratch_shapes=[
            pltpu.VMEM((rows, slots), jnp.bfloat16),
            pltpu.VMEM((rows * (D // BLK), BLK), jnp.float32),
            pltpu.VMEM((slots, BLK), jnp.float32),
            pltpu.VMEM((rows, BLK), jnp.float32),
        ],
        name="encode",
    )(mom, grad, thr, sel, sel, counts, fwd, inv)


MESH = pl.DeviceIdType.MESH


def copy_to(src, dst, send, recv, peer):
    return pltpu.make_async_remote_copy(
        src_ref=src, dst_ref=dst, send_sem=send, recv_sem=recv, device_id=peer, device_id_type=MESH
    )


CLASSES = 4
PIECES = 16


def exchange_kernel(
    reps, shards, mine, sel, param, inv, newparam, rowsout, total, scale, pbuf, cbuf, buf, send, recv, send2, recv2, local
):
    fetch = pltpu.make_async_copy(param, pbuf, local.at[0])
    fetch.start()
    s = lax.axis_index("shard")
    group = shards // 2
    core, far = lax.rem(s, 2), s // 2
    flip1 = lambda v: v + 1 - 2 * lax.rem(v, 2)
    flip2 = lambda v: v + 2 - 4 * lax.rem(v // 2, 2)
    inner = {"shard": flip1(s)}
    outer = [2 * lax.rem(far + k, group) + core for k in range(1, group)]

    me = lax.axis_index("dp")
    line, side = me // 2, lax.rem(me, 2)
    length = reps // 2
    rows, D = total.shape
    per_row = D // BLK
    slots = mine.shape[0]
    up, down, across = {"dp": me + 2}, {"dp": me - 2}, {"dp": me + 1 - 2 * side}
    has_up, has_down = line < length - 1, line > 0

    barrier = pltpu.get_barrier_semaphore()
    pl.semaphore_signal(barrier, inc=1, device_id=across, device_id_type=MESH)

    @pl.when(has_up)
    def _():
        pl.semaphore_signal(barrier, inc=1, device_id=up, device_id_type=MESH)

    @pl.when(has_down)
    def _():
        pl.semaphore_signal(barrier, inc=1, device_id=down, device_id_type=MESH)

    for peer in [inner] + [{"shard": o} for o in outer]:
        pl.semaphore_signal(barrier, inc=1, device_id=peer, device_id_type=MESH)
    pl.semaphore_wait(barrier, 2 + len(outer) + jnp.where(has_up, 1, 0) + jnp.where(has_down, 1, 0))

    def block(i, way, peer, own=False):
        src = mine if own else buf.at[i]
        return copy_to(src, buf.at[i], send.at[i, way], recv.at[i], peer)

    def first(act):
        @pl.when(has_up)
        def _():
            getattr(block(me, 0, up, True), act)()

        @pl.when(has_down)
        def _():
            getattr(block(me, 1, down, True), act)()

        getattr(block(me, 2, across, True), act)()

    def relay(d, act):
        @pl.when(line >= d)
        def _():
            i = me - 2 * d
            if act == "start":
                block(i, 0, across).wait_recv()

            @pl.when(has_up)
            def _():
                getattr(block(i, 0, up), act)()

            getattr(block(i, 2, across), act)()

        @pl.when(line + d < length)
        def _():
            i = me + 2 * d
            if act == "start":
                block(i, 1, across).wait_recv()

            @pl.when(has_down)
            def _():
                getattr(block(i, 1, down), act)()

            getattr(block(i, 2, across), act)()

    first("start")
    total[...] = jnp.zeros_like(total)
    batch = min(8, per_row // 2)

    def accumulate(i):
        ids = sel[i]
        col = ids % per_row
        hot = ids // per_row == lax.broadcasted_iota(jnp.int32, (rows, slots), 0)
        rowhot = jnp.where(hot, 1.0, 0.0).astype(jnp.bfloat16)
        odd = jnp.transpose(jnp.broadcast_to((col % 2).astype(jnp.float32), (BLK, slots)))
        right = odd.astype(jnp.bfloat16)
        values = buf[i]
        rhs = jnp.concatenate([values * (1.0 - odd).astype(jnp.bfloat16), values * right], axis=1)
        pair = jnp.broadcast_to(col // 2, (16, slots))

        def chunk(q, carry):
            parts = []
            for u in range(batch):
                pick = jnp.where(pair == q * batch + u, 1.0, 0.0).astype(jnp.bfloat16)
                parts.append(rowhot * jnp.concatenate([pick] * (rows // 16), axis=0))
            out = jnp.dot(jnp.concatenate(parts, axis=0), rhs, preferred_element_type=jnp.float32)
            for u in range(batch):
                at = pl.ds(pl.multiple_of((q * batch + u) * (2 * BLK), BLK), 2 * BLK)
                total[:, at] += out[u * rows : (u + 1) * rows]
            return carry

        lax.fori_loop(0, per_row // 2 // batch, chunk, 0)

    buf[me] = mine[...]

    def step(d, carry):
        @pl.when(d > 0)
        def _():
            relay(d, "start")

        def visit(t, carry):
            other = t // 2
            far = d - other
            at = line + (2 * lax.rem(t, 2) - 1) * far
            twin = (far == 0) & (lax.rem(t, 2) == 1)

            @pl.when((far >= 0) & (at >= 0) & (at < length) & jnp.logical_not(twin))
            def _():
                i = 2 * at + side + other * (1 - 2 * side)

                @pl.when(other == 1)
                def _():
                    block(i, 2, across).wait_recv()

                accumulate(i)

            return carry

        lax.fori_loop(0, 4, visit, 0)
        return carry

    lax.fori_loop(0, length + 1, step, 0)
    def square(c, acc):
        lanes = pl.ds(pl.multiple_of(c * BLK, BLK), BLK)
        a = total[:, lanes] * (1.0 / reps)
        total[:, lanes] = a
        return acc + a * a

    acc = lax.fori_loop(0, per_row, square, jnp.zeros((rows, BLK), jnp.float32), unroll=4)
    mean = jnp.sum(acc, axis=1, keepdims=True) * (1.0 / D)
    scale[...] = jnp.broadcast_to(lax.rsqrt(mean + 1e-06), scale.shape)
    fetch.wait()

    g = lax.rem(me, CLASSES)
    width = D // PIECES
    deep, side_peer = {"dp": flip2(me)}, across
    turns = PIECES // CLASSES

    def lanes(j):
        return pl.ds(pl.multiple_of(j * width, BLK), width)

    def piece(o, j, way, peer):
        ref = rowsout.at[o, :, lanes(j)]
        return copy_to(ref, ref, send2.at[o, j, way], recv2.at[o, j], peer)

    def own(j, k):
        return copy_to(
            cbuf.at[:, lanes(j)], rowsout.at[s, :, lanes(j)], send2.at[s, j, k], recv2.at[s, j], {"shard": outer[k]}
        )

    def compute(j):
        direction = both(split(tiles(total[:, lanes(j)])), inv[...])
        for c in range(width // BLK):
            at = pl.ds(pl.multiple_of(j * width + c * BLK, BLK), BLK)
            update = jnp.tanh(direction[c * rows : (c + 1) * rows] * scale[...])
            new = pbuf[:, at] - step_size * update
            pbuf[:, at] = new
            cbuf[:, at] = new.astype(jnp.bfloat16)

    def lead(k, carry):
        compute(g + CLASSES * k)

        @pl.when(k > 0)
        def _():
            for n in range(len(outer)):
                own(g + CLASSES * (k - 1), n).start()

        return carry

    def rest(turn):
        def one(k, carry):
            compute(lax.rem(g + turn, CLASSES) + CLASSES * k)
            return carry

        lax.fori_loop(0, turns, one, 0)

    sends = []

    def go(c):
        c.start()
        sends.append(c)

    lax.fori_loop(0, turns, lead, 0)
    rest(1)
    for n in range(len(outer)):
        own(g + CLASSES * (turns - 1), n).start()
        sends.extend(own(g + CLASSES * k, n) for k in range(turns))
    a, b, c = flip1(g), flip2(g), flip2(flip1(g))
    for k in range(turns):
        j = g + CLASSES * k
        for o in outer:
            piece(o, j, 0, inner).wait_recv()
            go(piece(o, j, 0, side_peer))
            go(piece(o, j, 1, deep))
            go(piece(o, j, 2, inner))
        if k < 2:
            rest(k + 2)
        if k == 1:
            store = pltpu.make_async_copy(pbuf, newparam, local.at[0])
            store.start()
        if k == 2:
            for direct in range(2, turns):
                for n in range(len(outer)):
                    go(own(c + CLASSES * direct, n))
    go(copy_to(cbuf, rowsout.at[s], send2.at[s, 0, group], recv2.at[s, PIECES], inner))
    keep = pltpu.make_async_copy(cbuf, rowsout.at[s], local.at[1])
    keep.start()
    for k in range(turns):
        for o in outer:
            j = a + CLASSES * k
            piece(o, j, 0, inner).wait_recv()
            if k == 0:
                go(piece(o, j, 1, deep))
            go(piece(o, j, 2, inner))
            j = b + CLASSES * k
            piece(o, j, 0, inner).wait_recv()
            if k == 1:
                go(piece(o, j, 0, side_peer))
            go(piece(o, j, 2, inner))
    for k in range(turns):
        for o in outer:
            piece(o, c + CLASSES * k, 0, inner).wait_recv()
            go(piece(o, c + CLASSES * k, 2, inner))
    other = flip1(s)
    copy_to(cbuf, rowsout.at[other], send2.at[other, 0, 0], recv2.at[other, PIECES], inner).wait_recv()
    for o in outer:
        for j in range(PIECES):
            piece(flip1(o), j, 0, inner).wait_recv()
    for x in sends:
        x.wait_send()
    first("wait_send")

    def drain(d, carry):
        relay(d, "wait_send")
        return carry

    lax.fori_loop(1, length, drain, 0)
    store.wait()
    keep.wait()


def exchange(sent, sel, param, inv, shards):
    reps = sel.shape[0]
    rows, D = param.shape
    vmem = pl.BlockSpec(memory_space=pltpu.VMEM)
    hbm = pl.BlockSpec(memory_space=pl.ANY)
    return pl.pallas_call(
        functools.partial(exchange_kernel, reps, shards),
        out_shape=[
            jax.ShapeDtypeStruct((rows, D), jnp.float32),
            jax.ShapeDtypeStruct((shards, rows, D), jnp.bfloat16),
        ],
        in_specs=[vmem, vmem, hbm, vmem],
        out_specs=[hbm, hbm],
        scratch_shapes=[
            pltpu.VMEM((rows, D), jnp.float32),
            pltpu.VMEM((rows, BLK), jnp.float32),
            pltpu.VMEM((rows, D), jnp.float32),
            pltpu.VMEM((rows, D), jnp.bfloat16),
            pltpu.VMEM((reps,) + sent.shape, sent.dtype),
            pltpu.SemaphoreType.DMA((reps, 3)),
            pltpu.SemaphoreType.DMA((reps,)),
            pltpu.SemaphoreType.DMA((shards, PIECES, max(3, shards))),
            pltpu.SemaphoreType.DMA((shards, PIECES + 1)),
            pltpu.SemaphoreType.DMA((2,)),
        ],
        compiler_params=pltpu.CompilerParams(collective_id=0, has_side_effects=True),
        name="exchange",
    )(sent, sel, param, inv)


def on_device(grads, momentum, param, thresholds, sel_blocks, counts):
    rows, D = param.shape
    width = min(1024, D)
    fwd, inv = (jnp.asarray(t) for t in tables())
    new_momentum, sent = encode(
        momentum[0], grads[0], thresholds[None, :], sel_blocks, counts[:, 0], fwd, inv, width
    )
    shards = lax.axis_size("shard")
    new_param, copies = exchange(sent, sel_blocks, param, inv, shards)
    compute_copy = copies.reshape(shards * rows, D)
    return (new_momentum[None], new_param, compute_copy)


def solution(mesh):
    placed = (
        P("dp", "shard", None),
        P("dp", "shard", None),
        P("shard", None),
        P("shard"),
        P(None, "shard", None),
        P(None, "shard"),
    )
    return jax.shard_map(
        on_device,
        mesh=mesh,
        in_specs=placed,
        out_specs=(P("dp", "shard", None), P("shard", None), P()),
        check_vma=False,
    )
```

profile of v0, /device:TPU:0, one launch (start us, length us, event | category | flops | bytes accessed | tf_op | source)
XLA Modules:
  0.0 72.2 jit_solution(2424024550378218167)
XLA Ops:
  0.6 12.0 %encode.1 = (f32[96,8192]{1,0:T(8,128)}, bf16[768,128]{1,0:T(8,128)(2,1)}) custom-call(f32[96,8192]{1,0:T(8,128)} %bitcast.7, bf16[96,8192]{1,0:T(8,128)(2,1)} %bitcast.8, f32[1,96]{1,0:T(1,128)} %bitcast.9, s32[8,1,768]{2,1,0:T(1,128)} %sel.3, s32[8,1,768]{2,1,0:T(1,128)} %sel.3, s32[8]{0:T(128)} %bitcast.10, bf16[256,256]{1,0:T(8,128)(2,1)} %constant.4.clone.fwd, ...), custom_call_target="tpu_custom_call" | custom-call | tf_op jit(solution)/shard_map/encode/pallas_call | solution.py:105
  12.6 52.0 %exchange.1 = (f32[96,8192]{1,0:T(8,128)}, bf16[4,96,8192]{2,1,0:T(8,128)(2,1)}) custom-call(bf16[768,128]{1,0:T(8,128)(2,1)} %get-tuple-element.8.mine, s32[8,1,768]{2,1,0:T(1,128)} %sel.3, f32[96,8192]{1,0:T(8,128)} %param.15, bf16[256,256]{1,0:T(8,128)(2,1)} %constant.5.clone.inv), custom_call_target="tpu_custom_call" | custom-call | tf_op jit(solution)/shard_map/exchange/pallas_call | solution.py:395
  64.7 0.0 copy-start
  64.7 3.9 %copy.13 = f32[96,8192]{1,0:T(8,128)} copy(f32[96,8192]{1,0:T(8,128)} %get-tuple-element.15) | data formatting | bytes 6291456
  68.6 1.0 %copy-done = bf16[4,96,8192]{2,1,0:T(8,128)(2,1)S(1)} copy-done((bf16[4,96,8192]{2,1,0:T(8,128)(2,1)S(1)}, bf16[4,96,8192]{2,1,0:T(8,128)(2,1)}, u32[]{:S(2)}) %copy-start) | copy-done | bytes 6291480
  69.5 2.7 %copy.14 = bf16[384,8192]{1,0:T(8,128)(2,1)} copy(bf16[384,8192]{1,0:T(8,128)(2,1)S(1)} %bitcast.6) | data formatting | bytes 12582912
Async XLA Ops:
  64.7 4.9 %copy-start = (bf16[4,96,8192]{2,1,0:T(8,128)(2,1)S(1)}, bf16[4,96,8192]{2,1,0:T(8,128)(2,1)}, u32[]{:S(2)}) copy-start(bf16[4,96,8192]{2,1,0:T(8,128)(2,1)} %get-tuple-element.10) | copy-start | bytes 18874372
where the time goes:
time: 72.6 us; the launch traced here: 72.2 us
  Pallas kernels  64 us (88%)
  local copies, waits for them, and re-layouts  7.56 us (10%)
    pallas_call x1, Pallas kernels, exchange(): pl.pallas_call(functools.partial(exchange_kernel, reps, shards), out_shap...  52 us
    pallas_call x1, Pallas kernels, encode(): pl.pallas_call(functools.partial(encode_kernel, D // BLK), grid=(D // wid...  12 us
    unnamed x4, local copies, waits for them, and re-layouts  7.56 us

commit v1 on v0

v1 whole, which is shorter than its diff:
```python
import functools

import jax
import jax.numpy as jnp
import numpy as np
from jax import lax
from jax.experimental import pallas as pl
from jax.experimental.pallas import tpu as pltpu
from jax.sharding import PartitionSpec as P

BLK = 128
HALF = 64
beta_decay = 0.999
step_size = 0.1
UNROLL = 16
CLASSES = 4
PIECES = 16
PARTS = 4
CHUNKS = 6
QUAD = 4


def tables():
    pos = np.arange(BLK)
    sample, freq = (pos % HALF)[:, None], (pos % HALF)[None, :]
    same = pos[:, None] // HALF == pos[None, :] // HALF
    weights = np.where(freq == 0, np.sqrt(1.0 / HALF), np.sqrt(2.0 / HALF))
    table = np.where(same, weights * np.cos((2 * sample + 1) * freq * (np.pi / BLK)), 0.0).astype(np.float32)

    def wide(t):
        hi = t.astype(jnp.bfloat16)
        lo = (t - hi.astype(np.float32)).astype(jnp.bfloat16)
        half = np.concatenate([hi, lo], axis=1)
        return np.concatenate([half, half], axis=0)

    return wide(table), wide(table.T)


def split(x):
    hi = x.astype(jnp.bfloat16)
    lo = (x - hi.astype(jnp.float32)).astype(jnp.bfloat16)
    return jnp.concatenate([hi, lo], axis=1)


def both(x, w):
    y = jnp.dot(x, w, preferred_element_type=jnp.float32)
    return y[:, :BLK] + y[:, BLK:]


def tiles(x):
    return jnp.concatenate([x[:, c * BLK : (c + 1) * BLK] for c in range(x.shape[1] // BLK)], axis=0)


MESH = pl.DeviceIdType.MESH


def copy_to(src, dst, send, recv, peer):
    return pltpu.make_async_remote_copy(
        src_ref=src, dst_ref=dst, send_sem=send, recv_sem=recv, device_id=peer, device_id_type=MESH
    )


def step_kernel(
    reps, shards, mom, grad, param, thr_in, sel_in, counts_in, fwd_in, inv_in,
    newmom, newparam, rowsout,
    flat, total, scale, gbuf, buf, picked, thr, sel, place, counts, fwd, inv,
    send, recv, send2, recv2, local, loads,
):
    s = lax.axis_index("shard")
    me = lax.axis_index("dp")
    rows, D = total.shape
    slots = buf.shape[1]
    per_row = D // BLK
    deep_rows = rows // CHUNKS

    def fetch(src, dst, k):
        c = pltpu.make_async_copy(src, dst, local.at[k])
        c.start()
        return c

    def load(c, act):
        at = pl.ds(pl.multiple_of(c * deep_rows, 16), deep_rows)
        getattr(pltpu.make_async_copy(mom.at[at], newmom.at[at], loads.at[c, 0]), act)()
        getattr(pltpu.make_async_copy(grad.at[at], gbuf.at[at], loads.at[c, 1]), act)()

    where = fetch(sel_in.at[me], place, 0)
    limits = fetch(thr_in, thr, 1)
    amounts = fetch(counts_in, counts, 6)
    for c in range(CHUNKS):
        load(c, "start")
    tables_in = [fetch(fwd_in, fwd, 2), fetch(inv_in, inv, 3), fetch(sel_in, sel, 4)]
    owned = fetch(param, newparam, 5)

    group = shards // 2
    core, far = lax.rem(s, 2), s // 2
    flip1 = lambda v: v + 1 - 2 * lax.rem(v, 2)
    flip2 = lambda v: v + 2 - 4 * lax.rem(v // 2, 2)
    inner = {"shard": flip1(s)}
    outer = [2 * lax.rem(far + k, group) + core for k in range(1, group)]

    line, side = me // 2, lax.rem(me, 2)
    length = reps // 2
    up, down, across = {"dp": me + 2}, {"dp": me - 2}, {"dp": me + 1 - 2 * side}
    deep = {"dp": flip2(me)}
    has_up, has_down = line < length - 1, line > 0

    barrier = pltpu.get_barrier_semaphore()
    pl.semaphore_signal(barrier, inc=1, device_id=across, device_id_type=MESH)

    @pl.when(has_up)
    def _():
        pl.semaphore_signal(barrier, inc=1, device_id=up, device_id_type=MESH)

    @pl.when(has_down)
    def _():
        pl.semaphore_signal(barrier, inc=1, device_id=down, device_id_type=MESH)

    for peer in [inner] + [{"shard": o} for o in outer]:
        pl.semaphore_signal(barrier, inc=1, device_id=peer, device_id_type=MESH)

    def blend(c, carry):
        load(c, "wait")
        for r in range(deep_rows // 16):
            at = pl.ds(pl.multiple_of(c * deep_rows + 16 * r, 16), 16)
            base = (c * deep_rows + 16 * r) * per_row
            for k in range(per_row):
                lanes = pl.ds(k * BLK, BLK)
                x = beta_decay * newmom[at, lanes] + gbuf[at, lanes].astype(jnp.float32)
                for h in range(2):
                    flat[pl.ds(pl.multiple_of(base + h * 8 * per_row + k * 8, 8), 8), :] = x[h * 8 : h * 8 + 8]
        return carry

    lax.fori_loop(0, CHUNKS, blend, 0)
    where.wait()
    limits.wait()
    amounts.wait()
    for c in tables_in:
        c.wait()

    run = slots // PARTS
    shift = per_row.bit_length() - 1
    assert per_row == 1 << shift

    def pick_part(p):
        def pick(i, carry):
            base = p * run + i * UNROLL
            got = []
            for u in range(UNROLL):
                b = place[0, base + u]
                row = lax.shift_right_logical(b, shift)
                tile = (row & -8) * per_row + (b & (per_row - 1)) * 8
                got.append(flat[pl.ds(tile + (row & 7), 1), :])
            for u in range(UNROLL):
                picked[pl.ds(base + u, 1), :] = got[u]
            return carry

        lax.fori_loop(0, run // UNROLL, pick, 0)

    def encode_part(p):
        at = pl.ds(p * run, run)
        coef = both(split(picked[at, :]), fwd[...])
        ids = sel[me][:, p * run : (p + 1) * run]
        row = jnp.transpose(jnp.broadcast_to((ids // per_row).astype(jnp.float32), (BLK, run)))[:, :rows]
        lane = lax.broadcasted_iota(jnp.int32, (run, rows), 1).astype(jnp.float32)
        t = jnp.sum(jnp.where(row == lane, thr[...], 0.0), axis=1, keepdims=True)
        shrunk = coef - jnp.clip(coef, -t, t)
        live = lax.broadcasted_iota(jnp.int32, (run, BLK), 0) + p * run < counts[me]
        buf[me, at, :] = jnp.where(live, shrunk, 0.0).astype(jnp.bfloat16)

    def block(i, p, way, peer):
        ref = buf.at[i, pl.ds(p * run, run)]
        return copy_to(ref, ref, send.at[i, p, way], recv.at[i, p], peer)

    def first(p, act):
        @pl.when(has_up)
        def _():
            getattr(block(me, p, 0, up), act)()

        @pl.when(has_down)
        def _():
            getattr(block(me, p, 1, down), act)()

        getattr(block(me, p, 2, across), act)()

    half = PARTS // 2

    def relay(d, p, act):
        @pl.when(line >= d)
        def _():
            i = me - 2 * d
            if act == "start":
                block(i, p, 0, across).wait_recv()

            @pl.when(has_up)
            def _():
                getattr(block(i, p, 0, up), act)()

            @pl.when((p < half) | (line > d))
            def _():
                getattr(block(i, p, 2, across), act)()

        @pl.when(line + d < length)
        def _():
            i = me + 2 * d
            if act == "start":
                block(i, p, 1, across).wait_recv()

            @pl.when(has_down)
            def _():
                getattr(block(i, p, 1, down), act)()

            @pl.when((p < half) | (line + d < length - 1))
            def _():
                getattr(block(i, p, 2, across), act)()

    def dual(f, act):
        @pl.when(line == f)
        def _():
            i = 1 - side
            for p in range(half, PARTS):
                if act == "start":
                    block(i, p, 0, across).wait_recv()

                @pl.when(has_up)
                def _():
                    getattr(block(i, p, 0, up), act)()

        @pl.when(line + f == length - 1)
        def _():
            i = 2 * (length - 1) + 1 - side
            for p in range(half, PARTS):
                if act == "start":
                    block(i, p, 1, across).wait_recv()

                @pl.when(has_down)
                def _():
                    getattr(block(i, p, 1, down), act)()

    def spread(i, fresh=False):
        ids = sel[i]
        col = ids % per_row
        hot = ids // per_row == lax.broadcasted_iota(jnp.int32, (rows, slots), 0)
        rowhot = jnp.where(hot, 1.0, 0.0).astype(jnp.bfloat16)
        sub = jnp.transpose(jnp.broadcast_to((col % QUAD).astype(jnp.float32), (BLK, slots)))
        values = buf[i]
        rhs = jnp.concatenate(
            [values * jnp.where(sub == float(g), 1.0, 0.0).astype(jnp.bfloat16) for g in range(QUAD)], axis=1
        )
        quad = jnp.broadcast_to(col // QUAD, (16, slots))
        parts = []
        for u in range(per_row // QUAD):
            pick = jnp.where(quad == u, 1.0, 0.0).astype(jnp.bfloat16)
            parts.append(rowhot * jnp.concatenate([pick] * (rows // 16), axis=0))
        out = jnp.dot(jnp.concatenate(parts, axis=0), rhs, preferred_element_type=jnp.float32)
        for u in range(per_row // QUAD):
            at = pl.ds(u * (QUAD * BLK), QUAD * BLK)
            if fresh:
                total[:, at] = out[u * rows : (u + 1) * rows]
            else:
                total[:, at] += out[u * rows : (u + 1) * rows]

    for p in range(PARTS):
        pick_part(p)
        if p == 1:
            arrivals = 2 + len(outer) + jnp.where(has_up, 1, 0) + jnp.where(has_down, 1, 0)
            pl.semaphore_wait(barrier, arrivals)
        if p > 0:
            first(p - 1, "start")
        encode_part(p)

    spread_width = D // PIECES

    def feed(j, carry):
        at = pl.ds(pl.multiple_of(j * spread_width, BLK), spread_width)
        x = both(tiles(total[:, at]).astype(jnp.bfloat16), inv[:BLK, :])
        for c in range(spread_width // BLK):
            k = j * (spread_width // BLK) + c
            lanes = pl.ds(pl.multiple_of(k * BLK, BLK), BLK)
            for r in range(rows // 8):
                old = flat[pl.ds(pl.multiple_of((r * per_row + k) * 8, 8), 8), :]
                newmom[pl.ds(r * 8, 8), lanes] = old - x[c * rows + r * 8 : c * rows + r * 8 + 8]
        return carry

    spread(me, True)
    first(PARTS - 1, "start")
    lax.fori_loop(0, PIECES, feed, 0)
    relay(1, 0, "start")
    relay(1, 1, "start")
    dual(0, "start")

    def step(d, carry):
        for p in range(half, PARTS):
            relay(d, p, "start")

        def turn(t, carry):
            other = t // 2
            away = d - other
            at = line + (2 * lax.rem(t, 2) - 1) * away
            twin = (away == 0) & (lax.rem(t, 2) == 1)

            @pl.when(t == 2)
            def _():
                relay(d + 1, 0, "start")

            @pl.when(t == 3)
            def _():
                relay(d + 1, 1, "start")
                dual(d, "start")

            @pl.when((at >= 0) & (at < length) & jnp.logical_not(twin))
            def _():
                i = 2 * at + side + other * (1 - 2 * side)

                @pl.when(other == 1)
                def _():
                    ends = (at == 0) | (at == length - 1)
                    for p in range(half):
                        block(i, p, 2, across).wait_recv()

                    @pl.when(jnp.logical_not(ends))
                    def _():
                        for p in range(half, PARTS):
                            block(i, p, 2, across).wait_recv()

                spread(i)

            return carry

        lax.fori_loop(0, 4, turn, 0)
        return carry

    lax.fori_loop(1, length + 1, step, 0)

    def square(c, acc):
        a = total[:, pl.ds(pl.multiple_of(c * BLK, BLK), BLK)]
        return acc + a * a

    acc = lax.fori_loop(0, per_row, square, jnp.zeros((rows, BLK), jnp.float32), unroll=8)
    mean = jnp.sum(acc, axis=1, keepdims=True) * (1.0 / (D * reps * reps))
    scale[...] = jnp.broadcast_to(lax.rsqrt(mean + 1e-06) * (1.0 / reps), scale.shape)
    owned.wait()

    g = lax.rem(me, CLASSES)
    width = D // PIECES
    turns = PIECES // CLASSES

    def lanes(j):
        return pl.ds(pl.multiple_of(j * width, BLK), width)

    def piece(o, j, way, peer):
        ref = rowsout.at[o, :, lanes(j)]
        return copy_to(ref, ref, send2.at[o, j, way], recv2.at[o, j], peer)

    def own(j, k):
        return piece(s, j, k, {"shard": outer[k]})

    def compute(j):
        direction = both(split(tiles(total[:, lanes(j)])), inv[...])
        for c in range(width // BLK):
            at = pl.ds(pl.multiple_of(j * width + c * BLK, BLK), BLK)
            update = jnp.tanh(direction[c * rows : (c + 1) * rows] * scale[...])
            new = newparam[:, at] - step_size * update
            newparam[:, at] = new
            rowsout[s, :, at] = new.astype(jnp.bfloat16)

    def lead(k, carry):
        compute(g + CLASSES * k)

        @pl.when(k > 0)
        def _():
            for n in range(len(outer)):
                own(g + CLASSES * (k - 1), n).start()

        return carry

    def rest(turn):
        def one(k, carry):
            compute(lax.rem(g + turn, CLASSES) + CLASSES * k)
            return carry

        lax.fori_loop(0, turns, one, 0)

    sends = []

    def go(c):
        c.start()
        sends.append(c)

    lax.fori_loop(0, turns, lead, 0)
    rest(1)
    for n in range(len(outer)):
        own(g + CLASSES * (turns - 1), n).start()
        sends.extend(own(g + CLASSES * k, n) for k in range(turns))
    a, b, c = flip1(g), flip2(g), flip2(flip1(g))
    for k in range(turns):
        j = g + CLASSES * k
        for o in outer:
            piece(o, j, 0, inner).wait_recv()
            go(piece(o, j, 0, across))
            go(piece(o, j, 1, deep))
            go(piece(o, j, 2, inner))
        if k < 2:
            rest(k + 2)
        if k == 2:
            for direct in range(2, turns):
                for n in range(len(outer)):
                    go(own(c + CLASSES * direct, n))
    go(copy_to(rowsout.at[s], rowsout.at[s], send2.at[s, 0, group], recv2.at[s, PIECES], inner))
    for k in range(turns):
        for o in outer:
            j = a + CLASSES * k
            piece(o, j, 0, inner).wait_recv()
            if k == 0:
                go(piece(o, j, 1, deep))
            go(piece(o, j, 2, inner))
            j = b + CLASSES * k
            piece(o, j, 0, inner).wait_recv()
            if k == 1:
                go(piece(o, j, 0, across))
            go(piece(o, j, 2, inner))
    for k in range(turns):
        for o in outer:
            piece(o, c + CLASSES * k, 0, inner).wait_recv()
            go(piece(o, c + CLASSES * k, 2, inner))
    other = flip1(s)
    copy_to(rowsout.at[other], rowsout.at[other], send2.at[other, 0, 0], recv2.at[other, PIECES], inner).wait_recv()
    for o in outer:
        for j in range(PIECES):
            piece(flip1(o), j, 0, inner).wait_recv()
    for x in sends:
        x.wait_send()
    for p in range(PARTS):
        first(p, "wait_send")

    def drain(d, carry):
        for p in range(PARTS):
            relay(d, p, "wait_send")
        return carry

    lax.fori_loop(1, length, drain, 0)

    def undual(f, carry):
        dual(f, "wait_send")
        return carry

    lax.fori_loop(0, length, undual, 0)


def step(mom, grad, param, thr, sel, counts, fwd, inv, shards):
    reps, _, slots = sel.shape
    rows, D = param.shape
    vmem = pl.BlockSpec(memory_space=pltpu.VMEM)
    hbm = pl.BlockSpec(memory_space=pltpu.HBM)
    dma = pltpu.SemaphoreType.DMA
    return pl.pallas_call(
        functools.partial(step_kernel, reps, shards),
        out_shape=[
            pltpu.VMEM((rows, D), jnp.float32),
            pltpu.VMEM((rows, D), jnp.float32),
            pltpu.VMEM((shards, rows, D), jnp.bfloat16),
        ],
        in_specs=[hbm] * 8,
        out_specs=[vmem, vmem, vmem],
        scratch_shapes=[
            pltpu.VMEM((rows * (D // BLK), BLK), jnp.float32),
            pltpu.VMEM((rows, D), jnp.float32),
            pltpu.VMEM((rows, BLK), jnp.float32),
            pltpu.VMEM((rows, D), jnp.bfloat16),
            pltpu.VMEM((reps, slots, BLK), jnp.bfloat16),
            pltpu.VMEM((slots, BLK), jnp.float32),
            pltpu.VMEM(thr.shape, jnp.float32),
            pltpu.VMEM(sel.shape, jnp.int32),
            pltpu.SMEM((1, slots), jnp.int32),
            pltpu.SMEM(counts.shape, jnp.int32),
            pltpu.VMEM(fwd.shape, fwd.dtype),
            pltpu.VMEM(inv.shape, inv.dtype),
            dma((reps, PARTS, 3)),
            dma((reps, PARTS)),
            dma((shards, PIECES, max(3, shards))),
            dma((shards, PIECES + 1)),
            dma((7,)),
            dma((CHUNKS, 2)),
        ],
        compiler_params=pltpu.CompilerParams(
            collective_id=0, has_side_effects=True, vmem_limit_bytes=36 * 1024 * 1024
        ),
        name="step",
    )(*[pltpu.with_memory_space_constraint(x, pltpu.HBM) for x in (mom, grad, param, thr, sel, counts, fwd, inv)])


def place_kernel(n, *refs):
    sems = refs[-1]
    copies = []
    for i in range(n):
        c = pltpu.make_async_copy(refs[i], refs[n + i], sems.at[i])
        c.start()
        copies.append(c)
    for c in copies:
        c.wait()


def place(*arrays):
    n = len(arrays)
    return pl.pallas_call(
        functools.partial(place_kernel, n),
        out_shape=[jax.ShapeDtypeStruct(a.shape, a.dtype) for a in arrays],
        in_specs=[pl.BlockSpec(memory_space=pltpu.VMEM)] * n,
        out_specs=[pl.BlockSpec(memory_space=pl.ANY)] * n,
        scratch_shapes=[pltpu.SemaphoreType.DMA((n,))],
        compiler_params=pltpu.CompilerParams(vmem_limit_bytes=1024 * 1024),
        name="place",
    )(*[pltpu.with_memory_space_constraint(a, pltpu.VMEM) for a in arrays])


def on_device(grads, momentum, param, thresholds, sel_blocks, counts):
    rows, D = param.shape
    fwd, inv = (jnp.asarray(t) for t in tables())
    shards = lax.axis_size("shard")
    outs = step(
        momentum[0], grads[0], param, thresholds[None, :], sel_blocks, counts[:, 0], fwd, inv, shards
    )
    new_momentum, new_param, copies = place(*outs)
    return (new_momentum[None], new_param, copies.reshape(shards * rows, D))


def solution(mesh):
    placed = (
        P("dp", "shard", None),
        P("dp", "shard", None),
        P("shard", None),
        P("shard"),
        P(None, "shard", None),
        P(None, "shard"),
    )
    return jax.shard_map(
        on_device,
        mesh=mesh,
        in_specs=placed,
        out_specs=(P("dp", "shard", None), P("shard", None), P()),
        check_vma=False,
    )
```

time: 72.6 us -> 58.3 us (0.80)
  local copies, waits for them, and re-layouts: 7.56 us -> 0 us
  Pallas kernels: 64 us -> 57.5 us
    unnamed x4 -> x0, local copies, waits for them, and re-layouts: 7.56 us -> none
    pallas_call x2, Pallas kernels: 64 us -> 57.5 us  [the longest x1 52.7 us: step(): pl.pallas_call(functools.partial(step_kernel, reps, shards), out_shape=[p...]
where the time goes in v1:
time: 58.3 us; the launch traced here: 58.1 us
  Pallas kernels  57.5 us (99%)
  between operations  0.64 us (1%)
    pallas_call x1, Pallas kernels, step(): pl.pallas_call(functools.partial(step_kernel, reps, shards), out_shape=[p...  52.7 us
    pallas_call x1, Pallas kernels, place(): pl.pallas_call(functools.partial(place_kernel, n), out_shape=[jax.ShapeDt...  4.8 us

profile of v1, /device:TPU:0, one launch (start us, length us, event | category | flops | bytes accessed | tf_op | source)
XLA Modules:
  0.0 58.1 jit_solution(11690419710079442599)
XLA Ops:
  0.6 52.7 %step.1 = (f32[96,8192]{1,0:T(8,128)S(1)}, f32[96,8192]{1,0:T(8,128)S(1)}, bf16[4,96,8192]{2,1,0:T(8,128)(2,1)S(1)}) custom-call(f32[96,8192]{1,0:T(8,128)} %bitcast.6, bf16[96,8192]{1,0:T(8,128)(2,1)} %bitcast.7, f32[96,8192]{1,0:T(8,128)} %param.15, f32[1,96]{1,0:T(1,128)} %bitcast.8, s32[8,1,768]{2,1,0:T(1,128)} %sel_in.1, s32[8]{0:T(128)} %bitcast.9, ...), custom_call_target="tpu_custom_call" | custom-call | tf_op jit(solution)/shard_map/step/pallas_call | solution.py:455
  53.3 4.8 %place.1 = (f32[96,8192]{1,0:T(8,128)}, f32[96,8192]{1,0:T(8,128)}, bf16[4,96,8192]{2,1,0:T(8,128)(2,1)}) custom-call(f32[96,8192]{1,0:T(8,128)S(1)} %get-tuple-element.9.refs_0_, f32[96,8192]{1,0:T(8,128)S(1)} %get-tuple-element.10.refs_1_, bf16[4,96,8192]{2,1,0:T(8,128)(2,1)S(1)} %get-tuple-element.11.refs_2_), custom_call_target="tpu_custom_call" | custom-call | tf_op jit(solution)/shard_map/place/pallas_call | solution.py:504

commit v2 on v1

--- a/solution.py
+++ b/solution.py
@@ -12,12 +12,14 @@
 HALF = 64
 beta_decay = 0.999
 step_size = 0.1
-UNROLL = 16
+UNROLL = 48
 CLASSES = 4
 PIECES = 16
 PARTS = 4
-CHUNKS = 6
+CHUNKS = 3
 QUAD = 4
+FEED = 16
+LAG = 2
 
 
 def tables():
@@ -63,8 +65,8 @@
 def step_kernel(
     reps, shards, mom, grad, param, thr_in, sel_in, counts_in, fwd_in, inv_in,
     newmom, newparam, rowsout,
-    flat, total, scale, gbuf, buf, picked, thr, sel, place, counts, fwd, inv,
-    send, recv, send2, recv2, local, loads,
+    flat, total, scale, gbuf, buf, picked, thr, sel, index, place, counts, fwd, inv,
+    along, below, sides, duals, recv, owns, hops_x, hops_z, passes, recv_far, recv_near, whole, local, loads,
 ):
     s = lax.axis_index("shard")
     me = lax.axis_index("dp")
@@ -83,13 +85,10 @@
         getattr(pltpu.make_async_copy(mom.at[at], newmom.at[at], loads.at[c, 0]), act)()
         getattr(pltpu.make_async_copy(grad.at[at], gbuf.at[at], loads.at[c, 1]), act)()
 
-    where = fetch(sel_in.at[me], place, 0)
-    limits = fetch(thr_in, thr, 1)
-    amounts = fetch(counts_in, counts, 6)
+    choices = fetch(sel_in, sel, 4)
     for c in range(CHUNKS):
         load(c, "start")
-    tables_in = [fetch(fwd_in, fwd, 2), fetch(inv_in, inv, 3), fetch(sel_in, sel, 4)]
-    owned = fetch(param, newparam, 5)
+    small = [fetch(thr_in, thr, 1), fetch(counts_in, counts, 6), fetch(fwd_in, fwd, 2), fetch(inv_in, inv, 3)]
 
     group = shards // 2
     core, far = lax.rem(s, 2), s // 2
@@ -130,26 +129,25 @@
                     flat[pl.ds(pl.multiple_of(base + h * 8 * per_row + k * 8, 8), 8), :] = x[h * 8 : h * 8 + 8]
         return carry
 
-    lax.fori_loop(0, CHUNKS, blend, 0)
+    choices.wait()
+    ids = sel[me]
+    row = ids // per_row
+    index[...] = (row // 8) * (8 * per_row) + (ids % per_row) * 8 + row % 8
+    blend(0, 0)
+    where = fetch(index, place, 0)
+    lax.fori_loop(1, CHUNKS, blend, 0)
+    owned = fetch(param, newparam, 5)
+    for c in small:
+        c.wait()
     where.wait()
-    limits.wait()
-    amounts.wait()
-    for c in tables_in:
-        c.wait()
-
     run = slots // PARTS
-    shift = per_row.bit_length() - 1
-    assert per_row == 1 << shift
 
     def pick_part(p):
         def pick(i, carry):
             base = p * run + i * UNROLL
             got = []
             for u in range(UNROLL):
-                b = place[0, base + u]
-                row = lax.shift_right_logical(b, shift)
-                tile = (row & -8) * per_row + (b & (per_row - 1)) * 8
-                got.append(flat[pl.ds(tile + (row & 7), 1), :])
+                got.append(flat[pl.ds(place[0, base + u], 1), :])
             for u in range(UNROLL):
                 picked[pl.ds(base + u, 1), :] = got[u]
             return carry
@@ -167,51 +165,54 @@
         live = lax.broadcasted_iota(jnp.int32, (run, BLK), 0) + p * run < counts[me]
         buf[me, at, :] = jnp.where(live, shrunk, 0.0).astype(jnp.bfloat16)
 
-    def block(i, p, way, peer):
+    half = PARTS // 2
+
+    def block(i, p, sem, peer):
         ref = buf.at[i, pl.ds(p * run, run)]
-        return copy_to(ref, ref, send.at[i, p, way], recv.at[i, p], peer)
+        return copy_to(ref, ref, sem, recv.at[i, p], peer)
+
+    def arrived(i, p):
+        block(i, p, below.at[p], across).wait_recv()
 
     def first(p, act):
         @pl.when(has_up)
         def _():
-            getattr(block(me, p, 0, up), act)()
+            getattr(block(me, p, along.at[line, p], up), act)()
 
         @pl.when(has_down)
         def _():
-            getattr(block(me, p, 1, down), act)()
-
-        getattr(block(me, p, 2, across), act)()
-
-    half = PARTS // 2
+            getattr(block(me, p, below.at[p], down), act)()
+
+        getattr(block(me, p, sides.at[line, p], across), act)()
 
     def relay(d, p, act):
         @pl.when(line >= d)
         def _():
-            i = me - 2 * d
+            i, at = me - 2 * d, line - d
             if act == "start":
-                block(i, p, 0, across).wait_recv()
+                arrived(i, p)
 
             @pl.when(has_up)
             def _():
-                getattr(block(i, p, 0, up), act)()
-
-            @pl.when((p < half) | (line > d))
-            def _():
-                getattr(block(i, p, 2, across), act)()
+                getattr(block(i, p, along.at[at, p], up), act)()
+
+            @pl.when((p < half) | (at > 0))
+            def _():
+                getattr(block(i, p, sides.at[at, p], across), act)()
 
         @pl.when(line + d < length)
         def _():
-            i = me + 2 * d
+            i, at = me + 2 * d, line + d
             if act == "start":
-                block(i, p, 1, across).wait_recv()
+                arrived(i, p)
 
             @pl.when(has_down)
             def _():
-                getattr(block(i, p, 1, down), act)()
-
-            @pl.when((p < half) | (line + d < length - 1))
-            def _():
-                getattr(block(i, p, 2, across), act)()
+                getattr(block(i, p, along.at[at, p], down), act)()
+
+            @pl.when((p < half) | (at < length - 1))
+            def _():
+                getattr(block(i, p, sides.at[at, p], across), act)()
 
     def dual(f, act):
         @pl.when(line == f)
@@ -219,22 +220,22 @@
             i = 1 - side
             for p in range(half, PARTS):
                 if act == "start":
-                    block(i, p, 0, across).wait_recv()
+                    arrived(i, p)
 
                 @pl.when(has_up)
                 def _():
-                    getattr(block(i, p, 0, up), act)()
+                    getattr(block(i, p, duals.at[0, p - half], up), act)()
 
         @pl.when(line + f == length - 1)
         def _():
             i = 2 * (length - 1) + 1 - side
             for p in range(half, PARTS):
                 if act == "start":
-                    block(i, p, 1, across).wait_recv()
+                    arrived(i, p)
 
                 @pl.when(has_down)
                 def _():
-                    getattr(block(i, p, 1, down), act)()
+                    getattr(block(i, p, duals.at[1, p - half], down), act)()
 
     def spread(i, fresh=False):
         ids = sel[i]
@@ -268,7 +269,7 @@
             first(p - 1, "start")
         encode_part(p)
 
-    spread_width = D // PIECES
+    spread_width = D // FEED
 
     def feed(j, carry):
         at = pl.ds(pl.multiple_of(j * spread_width, BLK), spread_width)
@@ -283,7 +284,7 @@
 
     spread(me, True)
     first(PARTS - 1, "start")
-    lax.fori_loop(0, PIECES, feed, 0)
+    lax.fori_loop(0, FEED, feed, 0)
     relay(1, 0, "start")
     relay(1, 1, "start")
     dual(0, "start")
@@ -315,12 +316,12 @@
                 def _():
                     ends = (at == 0) | (at == length - 1)
                     for p in range(half):
-                        block(i, p, 2, across).wait_recv()
+                        arrived(i, p)
 
                     @pl.when(jnp.logical_not(ends))
                     def _():
                         for p in range(half, PARTS):
-                            block(i, p, 2, across).wait_recv()
+                            arrived(i, p)
 
                 spread(i)
 
@@ -347,12 +348,22 @@
     def lanes(j):
         return pl.ds(pl.multiple_of(j * width, BLK), width)
 
-    def piece(o, j, way, peer):
-        ref = rowsout.at[o, :, lanes(j)]
-        return copy_to(ref, ref, send2.at[o, j, way], recv2.at[o, j], peer)
-
-    def own(j, k):
-        return piece(s, j, k, {"shard": outer[k]})
+    fan = range(len(outer))
+
+    def piece(n, j, sem, peer):
+        ref = rowsout.at[outer[n], :, lanes(j)]
+        return copy_to(ref, ref, sem, recv_far.at[n, j], peer)
+
+    def landed(n, j):
+        piece(n, j, whole.at[0], inner).wait_recv()
+
+    def beside(n, j):
+        ref = rowsout.at[outer[n], :, lanes(j)]
+        return copy_to(ref, ref, passes.at[n, j], recv_near.at[n, j], inner)
+
+    def own(j, k, n):
+        ref = rowsout.at[s, :, lanes(j)]
+        return copy_to(ref, ref, owns.at[n, k], recv_far.at[group - 2 - n, j], {"shard": outer[n]})
 
     def compute(j):
         direction = both(split(tiles(total[:, lanes(j)])), inv[...])
@@ -363,22 +374,33 @@
             newparam[:, at] = new
             rowsout[s, :, at] = new.astype(jnp.bfloat16)
 
+    a, b, c = flip1(g), flip2(g), flip2(flip1(g))
+    quarter = turns // 4
+
     def lead(k, carry):
         compute(g + CLASSES * k)
 
         @pl.when(k > 0)
         def _():
-            for n in range(len(outer)):
-                own(g + CLASSES * (k - 1), n).start()
+            for n in fan:
+                own(g + CLASSES * (k - 1), k - 1, n).start()
 
         return carry
 
-    def rest(turn):
-        def one(k, carry):
-            compute(lax.rem(g + turn, CLASSES) + CLASSES * k)
-            return carry
-
-        lax.fori_loop(0, turns, one, 0)
+    def follow(k, carry):
+        compute(c + CLASSES * k)
+
+        @pl.when(k == 0)
+        def _():
+            for n in fan:
+                own(g + CLASSES * (turns - 1), turns - 1, n).start()
+
+        @pl.when(k > 2 * quarter)
+        def _():
+            for n in fan:
+                own(c + CLASSES * (k - 1), turns + k - 1 - 2 * quarter, n).start()
+
+        return carry
 
     sends = []
 
@@ -387,46 +409,51 @@
         sends.append(c)
 
     lax.fori_loop(0, turns, lead, 0)
-    rest(1)
-    for n in range(len(outer)):
-        own(g + CLASSES * (turns - 1), n).start()
-        sends.extend(own(g + CLASSES * k, n) for k in range(turns))
-    a, b, c = flip1(g), flip2(g), flip2(flip1(g))
+    lax.fori_loop(0, turns, follow, 0)
+    for n in fan:
+        sends.extend(own(g + CLASSES * k, k, n) for k in range(turns))
+        sends.extend(own(c + CLASSES * k, turns + k - 2 * quarter, n) for k in range(2 * quarter, turns - 1))
+
+    def pass_on(k):
+        for n in fan:
+            j = a + CLASSES * k
+            landed(n, j)
+            if k < quarter:
+                go(piece(n, j, hops_z.at[n, turns + k], deep))
+            go(beside(n, j))
+            j = b + CLASSES * k
+            landed(n, j)
+            if quarter <= k < 2 * quarter:
+                go(piece(n, j, hops_x.at[n, turns + k - quarter], across))
+            go(beside(n, j))
+
     for k in range(turns):
         j = g + CLASSES * k
-        for o in outer:
-            piece(o, j, 0, inner).wait_recv()
-            go(piece(o, j, 0, across))
-            go(piece(o, j, 1, deep))
-            go(piece(o, j, 2, inner))
-        if k < 2:
-            rest(k + 2)
-        if k == 2:
-            for direct in range(2, turns):
-                for n in range(len(outer)):
-                    go(own(c + CLASSES * direct, n))
-    go(copy_to(rowsout.at[s], rowsout.at[s], send2.at[s, 0, group], recv2.at[s, PIECES], inner))
+        compute(a + CLASSES * k)
+        for n in fan:
+            landed(n, j)
+            go(piece(n, j, hops_x.at[n, k], across))
+            go(piece(n, j, hops_z.at[n, k], deep))
+            go(beside(n, j))
+        if k == 0:
+            for n in fan:
+                go(own(c + CLASSES * (turns - 1), 2 * turns - 1 - 2 * quarter, n))
+        compute(b + CLASSES * k)
+        if k >= LAG:
+            pass_on(k - LAG)
+    go(copy_to(rowsout.at[s], rowsout.at[s], whole.at[0], whole.at[1], inner))
+    for k in range(turns - LAG, turns):
+        pass_on(k)
     for k in range(turns):
-        for o in outer:
-            j = a + CLASSES * k
-            piece(o, j, 0, inner).wait_recv()
-            if k == 0:
-                go(piece(o, j, 1, deep))
-            go(piece(o, j, 2, inner))
-            j = b + CLASSES * k
-            piece(o, j, 0, inner).wait_recv()
-            if k == 1:
-                go(piece(o, j, 0, across))
-            go(piece(o, j, 2, inner))
-    for k in range(turns):
-        for o in outer:
-            piece(o, c + CLASSES * k, 0, inner).wait_recv()
-            go(piece(o, c + CLASSES * k, 2, inner))
+        for n in fan:
+            landed(n, c + CLASSES * k)
+            go(beside(n, c + CLASSES * k))
     other = flip1(s)
-    copy_to(rowsout.at[other], rowsout.at[other], send2.at[other, 0, 0], recv2.at[other, PIECES], inner).wait_recv()
-    for o in outer:
+    copy_to(rowsout.at[other], rowsout.at[other], whole.at[0], whole.at[1], inner).wait_recv()
+    for n in fan:
         for j in range(PIECES):
-            piece(flip1(o), j, 0, inner).wait_recv()
+            ref = rowsout.at[flip1(outer[n]), :, lanes(j)]
+            copy_to(ref, ref, passes.at[n, j], recv_near.at[n, j], inner).wait_recv()
     for x in sends:
         x.wait_send()
     for p in range(PARTS):
@@ -439,11 +466,15 @@
 
     lax.fori_loop(1, length, drain, 0)
 
-    def undual(f, carry):
-        dual(f, "wait_send")
-        return carry
-
-    lax.fori_loop(0, length, undual, 0)
+    for p in range(half, PARTS):
+
+        @pl.when(has_up)
+        def _():
+            block(1 - side, p, duals.at[0, p - half], up).wait_send()
+
+        @pl.when(has_down)
+        def _():
+            block(2 * (length - 1) + 1 - side, p, duals.at[1, p - half], down).wait_send()
 
 
 def step(mom, grad, param, thr, sel, counts, fwd, inv, shards):
@@ -470,14 +501,23 @@
             pltpu.VMEM((slots, BLK), jnp.float32),
             pltpu.VMEM(thr.shape, jnp.float32),
             pltpu.VMEM(sel.shape, jnp.int32),
+            pltpu.VMEM((1, slots), jnp.int32),
             pltpu.SMEM((1, slots), jnp.int32),
             pltpu.SMEM(counts.shape, jnp.int32),
             pltpu.VMEM(fwd.shape, fwd.dtype),
             pltpu.VMEM(inv.shape, inv.dtype),
-            dma((reps, PARTS, 3)),
+            dma((reps // 2, PARTS)),
+            dma((PARTS,)),
+            dma((reps // 2, PARTS)),
+            dma((2, PARTS // 2)),
             dma((reps, PARTS)),
-            dma((shards, PIECES, max(3, shards))),
-            dma((shards, PIECES + 1)),
+            dma((shards // 2 - 1, 3 * PIECES // CLASSES // 2)),
+            dma((shards // 2 - 1, 5 * PIECES // CLASSES // 4)),
+            dma((shards // 2 - 1, 5 * PIECES // CLASSES // 4)),
+            dma((shards // 2 - 1, PIECES)),
+            dma((shards // 2 - 1, PIECES)),
+            dma((shards // 2 - 1, PIECES)),
+            dma((2,)),
             dma((7,)),
             dma((CHUNKS, 2)),
         ],

time: 58.3 us -> 53.6 us (0.919)
  Pallas kernels: 57.5 us -> 52.8 us
    pallas_call x1, Pallas kernels: 52.7 us -> 48 us  [step(): pl.pallas_call(functools.partial(step_kernel, reps, shards), out_shape=[p...]
where the time goes in v2:
time: 53.6 us; the launch traced here: 53.4 us
  Pallas kernels  52.8 us (99%)
  between operations  0.64 us (1%)
    pallas_call x1, Pallas kernels, step(): pl.pallas_call(functools.partial(step_kernel, reps, shards), out_shape=[p...  48 us
    pallas_call x1, Pallas kernels, place(): pl.pallas_call(functools.partial(place_kernel, n), out_shape=[jax.ShapeDt...  4.8 us

profile of v2, /device:TPU:0, one launch (start us, length us, event | category | flops | bytes accessed | tf_op | source)
XLA Modules:
  0.0 53.4 jit_solution(16672681832302784631)
XLA Ops:
  0.6 48.0 %step.1 = (f32[96,8192]{1,0:T(8,128)S(1)}, f32[96,8192]{1,0:T(8,128)S(1)}, bf16[4,96,8192]{2,1,0:T(8,128)(2,1)S(1)}) custom-call(f32[96,8192]{1,0:T(8,128)} %bitcast.6, bf16[96,8192]{1,0:T(8,128)(2,1)} %bitcast.7, f32[96,8192]{1,0:T(8,128)} %param.15, f32[1,96]{1,0:T(1,128)} %bitcast.8, s32[8,1,768]{2,1,0:T(1,128)} %sel_in.1, s32[8]{0:T(128)} %bitcast.9, ...), custom_call_target="tpu_custom_call" | custom-call | tf_op jit(solution)/shard_map/step/pallas_call | solution.py:486
  48.6 4.8 %place.1 = (f32[96,8192]{1,0:T(8,128)}, f32[96,8192]{1,0:T(8,128)}, bf16[4,96,8192]{2,1,0:T(8,128)(2,1)}) custom-call(f32[96,8192]{1,0:T(8,128)S(1)} %get-tuple-element.9.refs_0_, f32[96,8192]{1,0:T(8,128)S(1)} %get-tuple-element.10.refs_1_, bf16[4,96,8192]{2,1,0:T(8,128)(2,1)S(1)} %get-tuple-element.11.refs_2_), custom_call_target="tpu_custom_call" | custom-call | tf_op jit(solution)/shard_map/place/pallas_call | solution.py:544
